TPU v7x, 32 devices: a whole 2x2x4 slice. The times are simulated.
32 devices in a mesh: fsdp: 16 (over z, y, x), tp: 2 (over core).
Axes of the slice: x: 2, y: 2, z: 4, core: 2. Of those that a mesh axis runs over, the one named last changes fastest.
Arguments:
- tokens: bfloat16 [4096, 896], P(('fsdp', 'tp')), may hold values from -6 to 6
- cotangent: bfloat16 [4096, 896], P(('fsdp', 'tp')), may hold values from -6 to 6
- parents: int32 [16, 2], P('fsdp'), may hold values from 0 to 0, as said below
- skip: int32 [16], P('fsdp'), may hold values 0 or 1
- w_query: bfloat16 [896, 896], P('fsdp', 'tp'), may hold values from -0.1875 to 0.1875
- key_matrix: bfloat16 [896, 128], P('fsdp', 'tp'), may hold values from -0.1875 to 0.1875
- value_matrix: bfloat16 [896, 128], P('fsdp', 'tp'), may hold values from -0.1875 to 0.1875
- w_out: bfloat16 [896, 896], P('tp', 'fsdp'), may hold values from -0.75 to 0.75
- w_gate: bfloat16 [896, 4864], P('fsdp', 'tp'), may hold values from -0.1875 to 0.1875
- w_up: bfloat16 [896, 4864], P('fsdp', 'tp'), may hold values from -0.1875 to 0.1875
- w_down: bfloat16 [4864, 896], P('tp', 'fsdp'), may hold values from -0.078125 to 0.078125
- gain_attn: bfloat16 [896], P('fsdp'), may hold values from 0.5 to 1.5
- gain_mlp: bfloat16 [896], P('fsdp'), may hold values from 0.5 to 1.5
Outputs:
- output: bfloat16 [4096, 896], P(('fsdp', 'tp'))
- grad_tokens: bfloat16 [4096, 896], P(('fsdp', 'tp'))
- grad_w_query: float32 [896, 896], P('fsdp', 'tp')
- grad_w_key: float32 [896, 128], P('fsdp', 'tp')
- grad_w_value: float32 [896, 128], P('fsdp', 'tp')
- grad_w_out: float32 [896, 896], P('tp', 'fsdp')
- grad_w_gate: float32 [896, 4864], P('fsdp', 'tp')
- grad_w_up: float32 [896, 4864], P('fsdp', 'tp')
- grad_w_down: float32 [4864, 896], P('tp', 'fsdp')
- grad_gain_attn: float32 [896], P('fsdp')
- grad_gain_mlp: float32 [896], P('fsdp')
Inputs may be any that keep to these rules, and one draw needn't show every extreme that they name: `parents`: block 0 of a tree is its own parent; each tree has two blocks, and block 1 has block 0 as its parent, so every tree's mask is causal and pos is the token's place in its tree.
All inputs are finite; a program needn't handle non-finite values. No bound on the sum of `skip` on one device may be relied on, other than what follows from the above.
Results may differ from a plain program's by a relative error of at most 0.015.
Values may be sent and summed in bfloat16 or wider, within the bound.
No kernel may reach another device: no remote copies, remote signals or barrier semaphores. Data moves between devices by JAX's collectives and lax.ppermute only.
A program may use at most 192 MiB of HBM per device.

v0:
```python
import jax
import jax.numpy as jnp
from jax import lax
from jax.sharding import PartitionSpec as P

HEAD_SIZE = 64
BLK = 128
eps = 1e-05
rotary_base = 10000.0


def cut_along(value, dim, peers):
    shape = value.shape
    pieces = value.reshape(*shape[:dim], peers, shape[dim] // peers, *shape[dim + 1 :])
    return jnp.moveaxis(pieces, dim, 0)


def summed_on_arrival(value, axis, dim):
    peers = lax.axis_size(axis)
    pieces = lax.all_to_all(cut_along(value, dim, peers), axis, 0, 0, tiled=True)
    return jnp.sum(pieces.astype(jnp.float32), axis=0)


def tree_tables(parents, blocks, block_len):
    block_ids = jnp.arange(blocks, dtype=jnp.int32)
    ancestry = jnp.eye(blocks, dtype=jnp.float32)
    depths = jnp.zeros((blocks,), jnp.float32)
    picked = (block_ids == parents[1]).astype(jnp.float32)
    inherited = jnp.sum(picked[:, None] * ancestry, axis=0)
    ancestry = ancestry.at[1].set(jnp.maximum(ancestry[1], inherited))
    depths = depths.at[1].set(jnp.sum(picked * depths) + 1.0)
    token_ids = jnp.arange(blocks * block_len, dtype=jnp.int32)
    spread = jnp.repeat(jnp.repeat(ancestry, block_len, axis=0), block_len, axis=1)
    visible = (spread > 0.5) & (token_ids[None, :] <= token_ids[:, None])
    token_position = jnp.repeat(depths, block_len) * block_len + (token_ids % block_len).astype(
        jnp.float32
    )
    return (visible, token_position)


def apply_rotation(values, token_position, head_count, direction):
    count_of_rows = values.shape[0]
    shaped = values.reshape(count_of_rows, head_count, HEAD_SIZE)
    half_size = HEAD_SIZE // 2
    frequency = rotary_base ** (-2.0 * jnp.arange(half_size, dtype=jnp.float32) / HEAD_SIZE)
    angles = token_position[:, None] * frequency[None, :]
    cosine = jnp.cos(angles)[:, None, :]
    sine_part = direction * jnp.sin(angles)[:, None, :]
    first_half = shaped[..., :half_size]
    second_half = shaped[..., half_size:]
    turned = jnp.concatenate(
        [
            first_half * cosine - second_half * sine_part,
            second_half * cosine + first_half * sine_part,
        ],
        axis=-1,
    )
    return turned.reshape(count_of_rows, head_count * HEAD_SIZE)


def fetch_attention(w_query, key_matrix, value_matrix, w_out, gain_attn):
    return (
        lax.all_gather(w_query, "fsdp", axis=0, tiled=True),
        lax.all_gather(key_matrix, "fsdp", axis=0, tiled=True),
        lax.all_gather(value_matrix, "fsdp", axis=0, tiled=True),
        lax.all_gather(w_out, "fsdp", axis=1, tiled=True),
        lax.all_gather(gain_attn, "fsdp", axis=0, tiled=True),
    )


def fetch_mlp(w_gate, w_up, w_down, gain_mlp):
    return (
        lax.all_gather(w_gate, "fsdp", axis=0, tiled=True),
        lax.all_gather(w_up, "fsdp", axis=0, tiled=True),
        lax.all_gather(w_down, "fsdp", axis=1, tiled=True),
        lax.all_gather(gain_mlp, "fsdp", axis=0, tiled=True),
    )


def rows_inner(first_array, second_array):
    return lax.dot_general(
        first_array, second_array, (((0,), (0,)), ((), ())), preferred_element_type=jnp.float32
    )


def against(first_array, second_array):
    return lax.dot_general(
        first_array, second_array, (((1,), (1,)), ((), ())), preferred_element_type=jnp.float32
    )


def norm_back(grad_normed, scaled, statistic, gain_vector):
    grad_scaled = grad_normed * gain_vector
    return statistic * (
        grad_scaled - scaled * jnp.mean(grad_scaled * scaled, axis=-1, keepdims=True)
    )


def on_device(
    tokens,
    cotangent,
    parents,
    skip,
    w_query,
    key_matrix,
    value_matrix,
    w_out,
    w_gate,
    w_up,
    w_down,
    gain_attn,
    gain_mlp,
):
    half_rows = tokens.shape[0]
    seq_len = half_rows * lax.axis_size("tp")
    blocks = seq_len // BLK
    shard_rows = w_query.shape[0]
    heads_here = w_query.shape[1] // HEAD_SIZE
    kv_here = key_matrix.shape[1] // HEAD_SIZE
    heads_per_group = heads_here // kv_here
    query_cols = heads_here * HEAD_SIZE
    kv_cols = kv_here * HEAD_SIZE
    ff_here = w_gate.shape[1]
    score_scale = HEAD_SIZE ** (-0.5)
    visible, token_position = tree_tables(parents[0], blocks, BLK)
    active = (1 - skip[0]).astype(jnp.float32)
    query_all, key_all, value_all, out_all, gain_one = fetch_attention(
        w_query, key_matrix, value_matrix, w_out, gain_attn
    )
    inputs = tokens.astype(jnp.float32)
    stat_one = lax.rsqrt(jnp.mean(inputs * inputs, axis=-1, keepdims=True) + eps)
    scaled_one = inputs * stat_one
    gain_one_wide = gain_one.astype(jnp.float32)
    normed_input = (scaled_one * gain_one_wide).astype(jnp.bfloat16)
    normed_all = lax.all_gather(normed_input, "tp", axis=0, tiled=True)
    query_rows = apply_rotation(
        jnp.dot(normed_all, query_all, preferred_element_type=jnp.float32),
        token_position,
        heads_here,
        1.0,
    ).astype(jnp.bfloat16)
    key_row_block = apply_rotation(
        jnp.dot(normed_all, key_all, preferred_element_type=jnp.float32),
        token_position,
        kv_here,
        1.0,
    ).astype(jnp.bfloat16)
    value_row_block = jnp.dot(normed_all, value_all, preferred_element_type=jnp.float32).astype(
        jnp.bfloat16
    )
    query_per_head = query_rows.reshape(seq_len, kv_here, heads_per_group, HEAD_SIZE)
    key_per_head = key_row_block.reshape(seq_len, kv_here, HEAD_SIZE)
    value_per_head = value_row_block.reshape(seq_len, kv_here, HEAD_SIZE)

    def score_table():
        raw_scores = (
            jnp.einsum(
                "qhgd,khd->hgqk", query_per_head, key_per_head, preferred_element_type=jnp.float32
            )
            * score_scale
        )
        return jnp.where(visible, raw_scores, -1e30)

    scores = score_table()
    row_max = jnp.max(scores, axis=-1, keepdims=True)
    exponent = jnp.exp(scores - row_max)
    row_total = jnp.sum(exponent, axis=-1, keepdims=True)
    log_total = row_max + jnp.log(row_total)
    probs_low = (exponent / row_total).astype(jnp.bfloat16)
    attended = jnp.einsum(
        "hgqk,khd->qhgd", probs_low, value_per_head, preferred_element_type=jnp.float32
    )
    attended = attended.reshape(seq_len, query_cols).astype(jnp.bfloat16)
    branch = lax.psum_scatter(
        jnp.dot(attended, out_all, preferred_element_type=jnp.float32).astype(jnp.bfloat16),
        "tp",
        scatter_dimension=0,
        tiled=True,
    ).astype(jnp.float32)
    middle = inputs + active * branch
    gate_all, up_all, down_all, gain_two = fetch_mlp(w_gate, w_up, w_down, gain_mlp)
    stat_two = lax.rsqrt(jnp.mean(middle * middle, axis=-1, keepdims=True) + eps)
    scaled_two = middle * stat_two
    gain_two_wide = gain_two.astype(jnp.float32)
    normed_mlp = (scaled_two * gain_two_wide).astype(jnp.bfloat16)
    normed_mlp_all = lax.all_gather(normed_mlp, "tp", axis=0, tiled=True)
    gate_sum = jnp.dot(normed_mlp_all, gate_all, preferred_element_type=jnp.float32)
    upward = jnp.dot(normed_mlp_all, up_all, preferred_element_type=jnp.float32)
    sigmoid_gate = jax.nn.sigmoid(gate_sum)
    hidden = (gate_sum * sigmoid_gate * upward).astype(jnp.bfloat16)
    mlp_result = lax.psum_scatter(
        jnp.dot(hidden, down_all, preferred_element_type=jnp.float32).astype(jnp.bfloat16),
        "tp",
        scatter_dimension=0,
        tiled=True,
    ).astype(jnp.float32)
    output = (middle + active * mlp_result).astype(jnp.bfloat16)
    grad_out = cotangent.astype(jnp.float32)
    grad_mlp = (active * grad_out).astype(jnp.bfloat16)
    grad_mlp_all = lax.all_gather(grad_mlp, "tp", axis=0, tiled=True)
    gate_all, up_all, down_all, gain_two = fetch_mlp(w_gate, w_up, w_down, gain_mlp)
    gain_two_wide = gain_two.astype(jnp.float32)
    grad_hidden = against(grad_mlp_all, down_all)
    grad_gate = (
        grad_hidden * upward * sigmoid_gate * (1.0 + gate_sum * (1.0 - sigmoid_gate))
    ).astype(jnp.bfloat16)
    grad_up = (grad_hidden * gate_sum * sigmoid_gate).astype(jnp.bfloat16)
    grad_normed_mlp = lax.psum_scatter(
        (against(grad_gate, gate_all) + against(grad_up, up_all)).astype(jnp.bfloat16),
        "tp",
        scatter_dimension=0,
        tiled=True,
    ).astype(jnp.float32)
    column_part = normed_mlp_all
    grad_part = grad_mlp_all
    mlp_grads = lax.psum_scatter(
        jnp.concatenate(
            [
                rows_inner(column_part, grad_gate),
                rows_inner(column_part, grad_up),
                rows_inner(grad_part, hidden),
            ],
            axis=1,
        ),
        "fsdp",
        scatter_dimension=0,
        tiled=True,
    )
    grad_gain_two = jnp.sum(grad_normed_mlp * scaled_two, axis=0)
    grad_middle = grad_out + norm_back(grad_normed_mlp, scaled_two, stat_two, gain_two_wide)
    grad_branch = (active * grad_middle).astype(jnp.bfloat16)
    grad_branch_all = lax.all_gather(grad_branch, "tp", axis=0, tiled=True)
    query_all, key_all, value_all, out_all, gain_one = fetch_attention(
        w_query, key_matrix, value_matrix, w_out, gain_attn
    )
    gain_one_wide = gain_one.astype(jnp.float32)
    grad_attended = (
        against(grad_branch_all, out_all)
        .astype(jnp.bfloat16)
        .reshape(seq_len, kv_here, heads_per_group, HEAD_SIZE)
    )
    probs = jnp.exp(score_table() - log_total)
    probs_low = probs.astype(jnp.bfloat16)
    grad_probs = jnp.einsum(
        "qhgd,khd->hgqk", grad_attended, value_per_head, preferred_element_type=jnp.float32
    )
    grad_value = jnp.einsum(
        "hgqk,qhgd->khd", probs_low, grad_attended, preferred_element_type=jnp.float32
    )
    grad_value = grad_value.reshape(seq_len, kv_cols).astype(jnp.bfloat16)
    grad_scores = (
        probs * (grad_probs - jnp.sum(probs * grad_probs, axis=-1, keepdims=True))
    ).astype(jnp.bfloat16)
    grad_query = (
        jnp.einsum(
            "hgqk,khd->qhgd", grad_scores, key_per_head, preferred_element_type=jnp.float32
        ).reshape(seq_len, query_cols)
        * score_scale
    )
    grad_key = (
        jnp.einsum(
            "hgqk,qhgd->khd", grad_scores, query_per_head, preferred_element_type=jnp.float32
        ).reshape(seq_len, kv_cols)
        * score_scale
    )
    grad_query = apply_rotation(grad_query, token_position, heads_here, -1.0).astype(jnp.bfloat16)
    grad_key = apply_rotation(grad_key, token_position, kv_here, -1.0).astype(jnp.bfloat16)
    first_term = against(grad_query, query_all)
    second_term = against(grad_key, key_all)
    third_term = against(grad_value, value_all)
    grad_normed = lax.psum_scatter(
        (first_term + second_term + third_term).astype(jnp.bfloat16),
        "tp",
        scatter_dimension=0,
        tiled=True,
    ).astype(jnp.float32)
    column_part = normed_all
    grad_part = grad_branch_all
    attn_grads = summed_on_arrival(
        jnp.concatenate(
            [
                rows_inner(column_part, grad_query),
                rows_inner(column_part, grad_key),
                rows_inner(column_part, grad_value),
                rows_inner(grad_part, attended),
            ],
            axis=1,
        ).astype(jnp.bfloat16),
        "fsdp",
        0,
    )
    grad_gain_one = jnp.sum(grad_normed * scaled_one, axis=0)
    grad_tokens = (
        grad_middle + norm_back(grad_normed, scaled_one, stat_one, gain_one_wide)
    ).astype(jnp.bfloat16)
    gain_total_one, gain_total_two = lax.psum((grad_gain_one, grad_gain_two), ("fsdp", "tp"))
    offset = lax.axis_index("fsdp") * shard_rows
    grad_gain_attn = lax.dynamic_slice_in_dim(gain_total_one, offset, shard_rows)
    grad_gain_mlp = lax.dynamic_slice_in_dim(gain_total_two, offset, shard_rows)
    grad_w_query = attn_grads[:, :query_cols]
    grad_w_key = attn_grads[:, query_cols : query_cols + kv_cols]
    grad_w_value = attn_grads[:, query_cols + kv_cols : query_cols + 2 * kv_cols]
    grad_w_out = attn_grads[:, query_cols + 2 * kv_cols :].T
    grad_w_gate = mlp_grads[:, :ff_here]
    grad_w_up = mlp_grads[:, ff_here : 2 * ff_here]
    grad_w_down = mlp_grads[:, 2 * ff_here :].T
    return (
        output,
        grad_tokens,
        grad_w_query,
        grad_w_key,
        grad_w_value,
        grad_w_out,
        grad_w_gate,
        grad_w_up,
        grad_w_down,
        grad_gain_attn,
        grad_gain_mlp,
    )


def solution(mesh):
    in_specs = (
        P(("fsdp", "tp"), None),
        P(("fsdp", "tp"), None),
        P("fsdp", None),
        P("fsdp"),
        P("fsdp", "tp"),
        P("fsdp", "tp"),
        P("fsdp", "tp"),
        P("tp", "fsdp"),
        P("fsdp", "tp"),
        P("fsdp", "tp"),
        P("tp", "fsdp"),
        P("fsdp"),
        P("fsdp"),
    )
    out_specs = (
        P(("fsdp", "tp"), None),
        P(("fsdp", "tp"), None),
        P("fsdp", "tp"),
        P("fsdp", "tp"),
        P("fsdp", "tp"),
        P("tp", "fsdp"),
        P("fsdp", "tp"),
        P("fsdp", "tp"),
        P("tp", "fsdp"),
        P("fsdp"),
        P("fsdp"),
    )
    return jax.shard_map(
        on_device, mesh=mesh, in_specs=in_specs, out_specs=out_specs, check_vma=False
    )
```

profile of v0, /device:TPU:0, one launch (start us, length us, event | category | flops | bytes accessed | tf_op | source)
XLA Modules:
  0.0 1254.3 jit_solution(5714153399740913930)
XLA Ops:
  8.1 1.2 slice.77
  10.1 1.1 fusion.34
  11.5 1.3 fusion.70
  13.4 0.8 dynamic-update-slice.6
  14.3 0.8 dynamic-update-slice.5
  15.1 44.2 %all-reduce.4 = (bf16[896]{0:T(1024)(128)(2,1)}, bf16[896]{0:T(1024)(128)(2,1)S(1)}) all-reduce(bf16[896]{0:T(1024)(128)(2,1)S(1)} %dynamic-update-slice.6, bf16[896]{0:T(1024)(128)(2,1)S(1)} %dynamic-update-slice.5), channel_id=1, replica_groups=mesh['fsdp'=16,'tp'=2] {'fsdp'}, use_global_device_ids=true, to_apply=%add.1 | all-reduce | flops 1792 | bytes 7168
  59.4 37.0 %all_gather.51 = bf16[896,64]{1,0:T(8,128)(2,1)S(1)} all-gather(bf16[56,64]{1,0:T(8,128)(2,1)} %param.22), channel_id=1, replica_groups=mesh['fsdp'=16,'tp'=2] {'fsdp'}, dimensions={0}, use_global_device_ids=true | all-gather | bytes 121856 | tf_op jit(solution)/shard_map/all_gather | solution.py:64
  96.4 38.9 %all_gather.50 = bf16[896,64]{1,0:T(8,128)(2,1)S(1)} all-gather(bf16[56,64]{1,0:T(8,128)(2,1)} %param.23), channel_id=1, replica_groups=mesh['fsdp'=16,'tp'=2] {'fsdp'}, dimensions={0}, use_global_device_ids=true | all-gather | bytes 121856 | tf_op jit(solution)/shard_map/all_gather | solution.py:65
  135.3 1.1 fusion.31
  136.5 2.1 all_gather.49
  139.2 0.8 broadcast_multiply_fusion
  140.3 40.7 %all_gather.52 = bf16[896,448]{1,0:T(8,128)(2,1)S(1)} all-gather(bf16[56,448]{1,0:T(8,128)(2,1)S(1)} %copy-done.37), channel_id=1, replica_groups=mesh['fsdp'=16,'tp'=2] {'fsdp'}, dimensions={0}, use_global_device_ids=true | all-gather | bytes 852992 | tf_op jit(solution)/shard_map/all_gather | solution.py:63
  181.5 43.4 %all_gather.53 = bf16[448,896]{0,1:T(8,128)(2,1)S(1)} all-gather(bf16[448,56]{0,1:T(8,128)(2,1)S(1)} %copy-done.38), channel_id=1, replica_groups=mesh['fsdp'=16,'tp'=2] {'fsdp'}, dimensions={1}, use_global_device_ids=true | all-gather | bytes 852992 | tf_op jit(solution)/shard_map/all_gather | solution.py:66
  226.4 0.7 copy-done.18
  227.1 1.2 convolution_convert_fusion.3
  230.8 1.3 convert_element_type.213
  232.1 1.0 fusion.29
  233.1 2.3 all_gather.59
  235.3 1.3 log_add_fusion
  236.7 1.1 multiply_reduce_fusion
  238.4 1.1 multiply_convert_fusion.4
  239.4 2.3 all_gather.55
  241.7 63.3 %all-gather.6.cloned.1.call-done = bf16[896,2432]{1,0:T(8,128)(2,1)} async-done(((bf16[56,2432]{1,0:T(8,128)(2,1)}), bf16[896,2432]{1,0:T(8,128)(2,1)}) %all-gather.6.cloned.1.call-update) | async-done | bytes 4358160 | tf_op jit(solution)/shard_map/all_gather | solution.py:74
  305.1 5.3 fusion.74
  310.4 73.4 %all-gather.4.cloned.1.call-done = bf16[896,2432]{1,0:T(8,128)(2,1)} async-done(((bf16[56,2432]{1,0:T(8,128)(2,1)}), bf16[896,2432]{1,0:T(8,128)(2,1)}) %all-gather.4.cloned.1.call-update) | async-done | bytes 4358160 | tf_op jit(solution)/shard_map/all_gather | solution.py:73
  383.7 5.3 fusion.73
  389.1 73.4 %all-gather.8.cloned.1.call-done = bf16[2432,896]{0,1:T(8,128)(2,1)} async-done(((bf16[2432,56]{0,1:T(8,128)(2,1)}), bf16[2432,896]{0,1:T(8,128)(2,1)}) %all-gather.8.cloned.1.call-update) | async-done | bytes 4358160 | tf_op jit(solution)/shard_map/all_gather | solution.py:75
  462.4 6.9 multiply_convert_fusion
  469.3 1.5 fusion.75
  470.9 4.6 fusion.6
  475.7 6.3 fusion.78
  482.0 4.8 fusion.77
  486.9 2.0 fusion.30
  488.9 1.4 multiply_convert_fusion.3
  490.3 2.1 all_gather.60
  496.9 1.1 fusion.5
  498.1 4.6 convolution_convert_fusion.2
  502.7 4.8 fusion.79
  507.6 19.7 %pad_maximum_fusion = f32[896,7296]{1,0:T(8,128)} fusion(f32[896,2432]{1,0:T(8,128)} %fusion.79, f32[896,2432]{1,0:T(8,128)} %fusion.78, f32[896,2432]{1,0:T(8,128)} %fusion.77), kind=kLoop, calls=%fused_computation | loop fusion | flops 13074432 | bytes 52297728 | tf_op jit(solution)/shard_map/concatenate | solution.py:217
  527.5 0.8 copy-done.6
  529.9 2.1 pad_maximum_fusion.1
  532.0 4.4 all-to-all-start
  537.2 1.2 fusion.33
  538.4 106.9 %all-reduce.3 = (f32[896]{0:T(1024)S(1)}, f32[896]{0:T(1024)S(1)}) all-reduce(f32[896]{0:T(1024)S(1)} %get-tuple-element.37, f32[896]{0:T(1024)S(1)} %copy-done.41), channel_id=1, replica_groups=mesh['fsdp'=16,'tp'=2] {'fsdp','tp'}, use_global_device_ids=true, to_apply=%region_15.16 | all-reduce | flops 1792 | bytes 14336 | tf_op jit(solution)/shard_map/psum | solution.py:296
  646.6 2.2 fusion.26
  649.8 0.7 slice_bitcast_fusion
  650.5 593.5 %all-reduce.7.cloned.1.call-done = f32[896,7296]{1,0:T(8,128)} async-done(((f32[896,7296]{1,0:T(8,128)}), f32[896,7296]{1,0:T(8,128)}) %all-reduce.7.cloned.1.call-update) | async-done | bytes 26148880
  1244.0 2.9 dynamic-slice_bitcast_fusion
  (173 shorter events, 14.8 us)
Async XLA Ops:
  8.0 228.6 %reduce-scatter.5.cloned.1.call-start = ((), (), s32[]{:S(2)}) async-start(), calls=%async_computation.5 | async-start | bytes 688128 | tf_op jit(solution)/shard_map/reduce_scatter | solution.py:174
  8.1 131.9 %copy-start.46 = (f32[32]{0:T(128)}, f32[32]{0:T(128)S(1)}, u32[]{:S(2)}) copy-start(f32[32]{0:T(128)S(1)} %multiply_power_fusion) | copy-start | bytes 388
  8.1 131.9 %copy-start.42 = (f32[256]{0:T(256)}, f32[256]{0:T(256)S(1)}, u32[]{:S(2)}) copy-start(f32[256]{0:T(256)S(1)} %fusion.62) | copy-start | bytes 3076
  10.1 130.1 %copy-start.37 = (bf16[56,448]{1,0:T(8,128)(2,1)S(1)}, bf16[56,448]{1,0:T(8,128)(2,1)}, u32[]{:S(2)}) copy-start(bf16[56,448]{1,0:T(8,128)(2,1)} %param.21) | copy-start | bytes 150532
  11.2 124.1 %copy-start.48 = (f32[128]{0:T(128)}, f32[128]{0:T(128)S(1)}, u32[]{:S(2)}) copy-start(f32[128]{0:T(128)S(1)} %add_rsqrt_fusion.1) | copy-start | bytes 1540
  59.3 76.0 %copy-start.31 = (f32[896]{0:T(1024)}, f32[896]{0:T(1024)S(1)}, u32[]{:S(2)}) copy-start(f32[896]{0:T(1024)S(1)} %convert_element_type.200) | copy-start | bytes 10756
  96.4 43.6 %copy-start.12 = (bf16[896,64]{1,0:T(8,128)(2,1)}, bf16[896,64]{1,0:T(8,128)(2,1)S(1)}, u32[]{:S(2)}) copy-start(bf16[896,64]{1,0:T(8,128)(2,1)S(1)} %all_gather.51) | copy-start | bytes 344068
  135.3 45.7 %copy-start.10 = (bf16[896,64]{1,0:T(8,128)(2,1)}, bf16[896,64]{1,0:T(8,128)(2,1)S(1)}, u32[]{:S(2)}) copy-start(bf16[896,64]{1,0:T(8,128)(2,1)S(1)} %all_gather.50) | copy-start | bytes 344068
  138.9 86.9 %copy-start.27 = (bf16[256,64,1]{0,1,2:T(8,128)(2,1)}, bf16[256,64,1]{0,1,2:T(8,128)(2,1)S(1)}, u32[]{:S(2)}) copy-start(bf16[256,64,1]{0,1,2:T(8,128)(2,1)S(1)} %fusion.11) | copy-start | bytes 98308
  138.9 42.6 %copy-start.38 = (bf16[448,56]{0,1:T(8,128)(2,1)S(1)}, bf16[448,56]{0,1:T(8,128)(2,1)}, u32[]{:S(2)}) copy-start(bf16[448,56]{0,1:T(8,128)(2,1)} %param.24) | copy-start | bytes 150532
  140.0 84.9 %copy-start.24 = (f32[256,32]{0,1:T(8,128)}, f32[256,32]{0,1:T(8,128)S(1)}, u32[]{:S(2)}) copy-start(f32[256,32]{0,1:T(8,128)S(1)} %get-tuple-element.65) | copy-start | bytes 98308
  140.2 84.7 %copy-start.33 = (bf16[256,32]{0,1:T(8,128)(2,1)}, bf16[256,32]{0,1:T(8,128)(2,1)S(1)}, u32[]{:S(2)}) copy-start(bf16[256,32]{0,1:T(8,128)(2,1)S(1)} %get-tuple-element.61) | copy-start | bytes 49156
  140.2 84.7 %copy-start.35 = (bf16[256,32]{0,1:T(8,128)(2,1)}, bf16[256,32]{0,1:T(8,128)(2,1)S(1)}, u32[]{:S(2)}) copy-start(bf16[256,32]{0,1:T(8,128)(2,1)S(1)} %get-tuple-element.62) | copy-start | bytes 49156
  224.9 1.5 copy-start.1
  227.1 9.6 copy-start
  228.3 76.7 %all-gather.6.cloned.1.call-start = ((), (), s32[]{:S(2)}) async-start(), calls=%async_computation.7 | async-start | bytes 4630528 | tf_op jit(solution)/shard_map/all_gather | solution.py:74
  228.9 154.8 %all-gather.4.cloned.1.call-start = ((), (), s32[]{:S(2)}) async-start(), calls=%async_computation.6 | async-start | bytes 4630528 | tf_op jit(solution)/shard_map/all_gather | solution.py:73
  229.5 232.9 %all-gather.8.cloned.1.call-start = ((), (), s32[]{:S(2)}) async-start(), calls=%async_computation.8 | async-start | bytes 4630528 | tf_op jit(solution)/shard_map/all_gather | solution.py:75
  230.1 256.8 %reduce-scatter.9.cloned.1.call-start = ((), (), s32[]{:S(2)}) async-start(), calls=%async_computation.10 | async-start | bytes 688128 | tf_op jit(solution)/shard_map/reduce_scatter | solution.py:208
  462.4 6.9 copy-start.52
  469.3 1.6 copy-start.15
  469.3 1.6 copy-start.17
  475.5 61.7 %reduce-scatter.11.cloned.1.call-start = ((), (), s32[]{:S(2)}) async-start(), calls=%async_computation.11 | async-start | bytes 688128 | tf_op jit(solution)/shard_map/reduce_scatter | solution.py:271
  475.7 6.3 copy-start.3
  475.7 6.3 copy-start.16
  486.9 5.6 copy-start.2
  488.9 4.1 copy-start.26
  488.9 1.4 copy-start.50
  493.4 3.4 copy-start.22
  493.9 1.3 copy-start.34
  493.9 1.3 copy-start.36
  496.5 1.5 copy-start.14
  498.0 148.5 %reduce-scatter.7.cloned.1.call-start = ((), (), s32[]{:S(2)}) async-start(), calls=%async_computation.9 | async-start | bytes 688128 | tf_op jit(solution)/shard_map/reduce_scatter | solution.py:191
  498.1 4.6 copy-start.7
  507.5 736.5 %all-reduce.7.cloned.1.call-start = ((), (), s32[]{:S(2)}) async-start(), calls=%async_computation.12 | async-start | bytes 52297728
  527.3 1.0 copy-start.6
  527.3 1.5 copy-start.23
  528.3 1.2 copy-start.19
  532.0 5.2 copy-start.32
  532.0 5.2 copy-start.49
  532.0 6.4 copy-start.41
  532.0 114.5 %copy-start.4 = (bf16[128,896]{1,0:T(8,128)(2,1)S(1)}, bf16[128,896]{1,0:T(8,128)(2,1)}, u32[]{:S(2)}) copy-start(bf16[128,896]{1,0:T(8,128)(2,1)} %reduce-scatter.5.cloned.1.call-done) | copy-start | bytes 688132
  532.0 114.5 %copy-start.8 = (bf16[128,896]{1,0:T(8,128)(2,1)S(1)}, bf16[128,896]{1,0:T(8,128)(2,1)}, u32[]{:S(2)}) copy-start(bf16[128,896]{1,0:T(8,128)(2,1)} %param.18) | copy-start | bytes 688132
  532.0 114.5 %copy-start.9 = (bf16[128,896]{1,0:T(8,128)(2,1)S(1)}, bf16[128,896]{1,0:T(8,128)(2,1)}, u32[]{:S(2)}) copy-start(bf16[128,896]{1,0:T(8,128)(2,1)} %reduce-scatter.9.cloned.1.call-done) | copy-start | bytes 688132
  532.0 114.5 %copy-start.30 = (f32[896]{0:T(1024)S(1)}, f32[896]{0:T(1024)}, u32[]{:S(2)}) copy-start(f32[896]{0:T(1024)} %convert_element_type.213) | copy-start | bytes 10756
  532.0 114.5 %copy-start.45 = (f32[128]{0:T(128)S(1)}, f32[128]{0:T(128)}, u32[]{:S(2)}) copy-start(f32[128]{0:T(128)} %copy-done.44) | copy-start | bytes 1540
  532.0 114.5 %copy-start.51 = (f32[128]{0:T(128)S(1)}, f32[128]{0:T(128)}, u32[]{:S(2)}) copy-start(f32[128]{0:T(128)} %copy-done.50) | copy-start | bytes 1540
  532.0 116.7 %all-to-all-start = ((bf16[16,56,1024]{2,1,0:T(8,128)(2,1)}), bf16[16,56,1024]{2,1,0:T(8,128)(2,1)S(1)}, u32[]{:S(2)}, u32[]{:S(2)}) async-start(bf16[16,56,1024]{2,1,0:T(8,128)(2,1)} %pad_maximum_fusion.1), calls=%async_computation.4 | async-start | bytes 3670016 | tf_op jit(solution)/shard_map/all_to_all | solution.py:20
  (14 other events, 11.7 us)
Sparse Core Ops, SparseCore 0:
  228.5 3.9 reduce-scatter.4
  475.6 6.4 reduce-scatter.8
  498.1 6.5 reduce-scatter.10
  507.6 8.8 reduce-scatter.6
Sparse Core Ops, SparseCore 1:
  231.9 73.1 all-gather.5
  308.0 75.7 all-gather.3
  386.7 75.7 all-gather.7
  527.4 716.6 all-reduce.6
where the time goes:
time: 1260 us; the launch traced here: 1250 us
  waiting for transfers between devices  805 us (64%)
  blocking collectives  320 us (25%)
  matrix products  52.7 us (4%)
  other arithmetic  39.9 us (3%)
  between operations  18.2 us (1%)
  local copies, waits for them, and re-layouts  13.3 us (1%)
    unnamed x9, waiting for transfers between devices  595 us
    psum x1, blocking collectives, on_device(): lax.psum((grad_gain_one, grad_gain_two), ('fsdp', 'tp'))  107 us
    all_gather x1, waiting for transfers between devices, fetch_mlp(): lax.all_gather(w_gate, 'fsdp', axis=0, tiled=True)  73.4 us
    all_gather x1, waiting for transfers between devices, fetch_mlp(): lax.all_gather(w_down, 'fsdp', axis=1, tiled=True)  73.4 us
    all_gather x1, waiting for transfers between devices, fetch_mlp(): lax.all_gather(w_up, 'fsdp', axis=0, tiled=True)  63.3 us
    unnamed x1, blocking collectives  44.2 us
    all_gather x1, blocking collectives, fetch_attention(): lax.all_gather(w_out, 'fsdp', axis=1, tiled=True)  43.4 us
    all_gather x1, blocking collectives, fetch_attention(): lax.all_gather(w_query, 'fsdp', axis=0, tiled=True)  40.7 us
  transfers between devices with their start and end apart: 9, of which 4 were waited for; matrix products, arithmetic and copies ran while one was open for 5% of the time, Pallas kernels for 0%

commit v1 on v0

--- a/solution.py
+++ b/solution.py
@@ -7,6 +7,27 @@
 BLK = 128
 eps = 1e-05
 rotary_base = 10000.0
+
+
+def collect(value, axis, dim):
+    peers, index, extent = (lax.axis_size(axis), lax.axis_index(axis), value.shape[dim])
+    forward = [(i, (i + 1) % peers) for i in range(peers)]
+    left = [(i, (i - 1) % peers) for i in range(peers)]
+    result = jnp.zeros((*value.shape[:dim], peers * extent, *value.shape[dim + 1 :]), value.dtype)
+    result = lax.dynamic_update_slice_in_dim(result, value, index * extent, axis=dim)
+    from_left = from_right = value
+    half = peers // 2
+    for step in range(1, half + 1):
+        from_left = lax.ppermute(from_left, axis, forward)
+        result = lax.dynamic_update_slice_in_dim(
+            result, from_left, (index - step) % peers * extent, axis=dim
+        )
+        if step < peers - half:
+            from_right = lax.ppermute(from_right, axis, left)
+            result = lax.dynamic_update_slice_in_dim(
+                result, from_right, (index + step) % peers * extent, axis=dim
+            )
+    return result
 
 
 def cut_along(value, dim, peers):
@@ -60,7 +81,7 @@
 
 def fetch_attention(w_query, key_matrix, value_matrix, w_out, gain_attn):
     return (
-        lax.all_gather(w_query, "fsdp", axis=0, tiled=True),
+        collect(w_query, "fsdp", 0),
         lax.all_gather(key_matrix, "fsdp", axis=0, tiled=True),
         lax.all_gather(value_matrix, "fsdp", axis=0, tiled=True),
         lax.all_gather(w_out, "fsdp", axis=1, tiled=True),

time: 1260 us -> 1280 us (1.016)
  blocking collectives: 320 us -> 276 us
  starting transfers between devices: 4.91 us -> 44.2 us
  waiting for transfers between devices: 805 us -> 830 us
    all_gather x1 -> x0, blocking collectives: 40.7 us -> none  [fetch_attention(): lax.all_gather(w_query, 'fsdp', axis=0, tiled=True)]
    ppermute x0 -> x15, starting transfers between devices: none -> 39.4 us  [the longest x7 39.4 us: collect(): from_right = lax.ppermute(from_right, axis, left)]
    ppermute x0 -> x15, waiting for transfers between devices: none -> 25.3 us  [the longest x8 16.8 us: collect(): from_left = lax.ppermute(from_left, axis, forward)]
  transfers between devices with their start and end apart: 9 -> 24, of which waited for: 4 -> 15; matrix products, arithmetic and copies ran while one was open for 5% -> 6% of each run, Pallas kernels for 0% -> 0%
where the time goes in v1:
time: 1280 us
  waiting for transfers between devices  830 us (65%)
  blocking collectives  276 us (22%)
  matrix products  55 us (4%)
  starting transfers between devices  44.2 us (3%)
  other arithmetic  41.1 us (3%)
  between operations  18.5 us (1%)
  local copies, waits for them, and re-layouts  14 us (1%)
    unnamed x9, waiting for transfers between devices  595 us
    psum x1, blocking collectives, on_device(): lax.psum((grad_gain_one, grad_gain_two), ('fsdp', 'tp'))  107 us
    all_gather x1, waiting for transfers between devices, fetch_mlp(): lax.all_gather(w_down, 'fsdp', axis=1, tiled=True)  73.4 us
    all_gather x1, waiting for transfers between devices, fetch_mlp(): lax.all_gather(w_gate, 'fsdp', axis=0, tiled=True)  73.3 us
    all_gather x1, waiting for transfers between devices, fetch_mlp(): lax.all_gather(w_up, 'fsdp', axis=0, tiled=True)  63 us
    unnamed x1, blocking collectives  42.8 us
    all_gather x1, blocking collectives, fetch_attention(): lax.all_gather(w_out, 'fsdp', axis=1, tiled=True)  40.9 us
    ppermute x7, starting transfers between devices, collect(): from_right = lax.ppermute(from_right, axis, left)  39.4 us
  transfers between devices with their start and end apart: 24, of which 15 were waited for; matrix products, arithmetic and copies ran while one was open for 6% of the time, Pallas kernels for 0%

profile of v1, /device:TPU:0, one launch (start us, length us, event | category | flops | bytes accessed | tf_op | source)
XLA Modules:
  0.0 1278.7 jit_solution(391905807095752740)
XLA Ops:
  8.1 7.0 collective-permute-start.1
  18.4 1.3 fusion.73
  22.1 42.8 %all-reduce.4 = (bf16[896]{0:T(1024)(128)(2,1)}, bf16[896]{0:T(1024)(128)(2,1)S(1)}) all-reduce(bf16[896]{0:T(1024)(128)(2,1)S(1)} %dynamic-update-slice.6, bf16[896]{0:T(1024)(128)(2,1)S(1)} %dynamic-update-slice.5), channel_id=1, replica_groups=mesh['fsdp'=16,'tp'=2] {'fsdp'}, use_global_device_ids=true, to_apply=%add.1 | all-reduce | flops 1792 | bytes 7168
  64.9 37.0 %all_gather.47 = bf16[896,64]{1,0:T(8,128)(2,1)S(1)} all-gather(bf16[56,64]{1,0:T(8,128)(2,1)} %param.22), channel_id=1, replica_groups=mesh['fsdp'=16,'tp'=2] {'fsdp'}, dimensions={0}, use_global_device_ids=true | all-gather | bytes 121856 | tf_op jit(solution)/shard_map/all_gather | solution.py:85
  101.9 38.9 %all_gather.46 = bf16[896,64]{1,0:T(8,128)(2,1)S(1)} all-gather(bf16[56,64]{1,0:T(8,128)(2,1)} %param.23), channel_id=1, replica_groups=mesh['fsdp'=16,'tp'=2] {'fsdp'}, dimensions={0}, use_global_device_ids=true | all-gather | bytes 121856 | tf_op jit(solution)/shard_map/all_gather | solution.py:86
  141.9 2.1 all_gather.45
  146.9 40.9 %all_gather.48 = bf16[448,896]{0,1:T(8,128)(2,1)S(1)} all-gather(bf16[448,56]{0,1:T(8,128)(2,1)S(1)} %copy-done.36), channel_id=1, replica_groups=mesh['fsdp'=16,'tp'=2] {'fsdp'}, dimensions={1}, use_global_device_ids=true | all-gather | bytes 852992 | tf_op jit(solution)/shard_map/all_gather | solution.py:87
  188.8 2.9 collective-permute-start.3
  191.7 2.0 collective-permute-done.3
  193.7 5.8 collective-permute-start.5
  199.5 1.8 collective-permute-done.5
  201.3 5.9 collective-permute-start.7
  207.4 1.7 collective-permute-done.7
  209.1 5.9 collective-permute-start.9
  215.3 1.6 collective-permute-done.9
  216.9 5.9 collective-permute-start.11
  223.1 1.6 collective-permute-done.11
  224.6 5.9 collective-permute-start.13
  231.4 7.7 collective-permute-done.12
  239.2 7.7 collective-permute-done.14
  249.9 1.2 convolution_convert_fusion.3
  253.7 1.3 convert_element_type.213
  255.9 2.3 all_gather.54
  258.2 1.3 log_add_fusion
  262.2 2.4 all_gather.50
  264.7 63.0 %all-gather.6.cloned.1.call-done = bf16[896,2432]{1,0:T(8,128)(2,1)} async-done(((bf16[56,2432]{1,0:T(8,128)(2,1)}), bf16[896,2432]{1,0:T(8,128)(2,1)}) %all-gather.6.cloned.1.call-update) | async-done | bytes 4358160 | tf_op jit(solution)/shard_map/all_gather | solution.py:95
  327.7 5.3 fusion.77
  333.1 73.3 %all-gather.4.cloned.1.call-done = bf16[896,2432]{1,0:T(8,128)(2,1)} async-done(((bf16[56,2432]{1,0:T(8,128)(2,1)}), bf16[896,2432]{1,0:T(8,128)(2,1)}) %all-gather.4.cloned.1.call-update) | async-done | bytes 4358160 | tf_op jit(solution)/shard_map/all_gather | solution.py:94
  406.4 5.3 fusion.76
  411.7 73.4 %all-gather.8.cloned.1.call-done = bf16[2432,896]{0,1:T(8,128)(2,1)} async-done(((bf16[2432,56]{0,1:T(8,128)(2,1)}), bf16[2432,896]{0,1:T(8,128)(2,1)}) %all-gather.8.cloned.1.call-update) | async-done | bytes 4358160 | tf_op jit(solution)/shard_map/all_gather | solution.py:96
  485.1 6.9 multiply_convert_fusion
  492.0 1.5 fusion.78
  493.5 4.6 fusion.7
  498.2 6.3 fusion.80
  504.5 4.8 fusion.79
  509.3 1.9 fusion.31
  511.2 1.4 multiply_convert_fusion.3
  512.7 2.4 all_gather.55
  519.5 1.3 fusion.6
  520.8 5.0 convolution_convert_fusion.2
  525.8 6.1 fusion.81
  532.0 19.7 %pad_maximum_fusion = f32[896,7296]{1,0:T(8,128)} fusion(f32[896,2432]{1,0:T(8,128)} %fusion.81, f32[896,2432]{1,0:T(8,128)} %fusion.80, f32[896,2432]{1,0:T(8,128)} %fusion.79), kind=kLoop, calls=%fused_computation | loop fusion | flops 13074432 | bytes 52297728 | tf_op jit(solution)/shard_map/concatenate | solution.py:238
  554.3 2.1 pad_maximum_fusion.1
  556.5 4.4 all-to-all-start
  562.8 107.0 %all-reduce.3 = (f32[896]{0:T(1024)S(1)}, f32[896]{0:T(1024)S(1)}) all-reduce(f32[896]{0:T(1024)S(1)} %get-tuple-element.37, f32[896]{0:T(1024)S(1)} %copy-done.39), channel_id=1, replica_groups=mesh['fsdp'=16,'tp'=2] {'fsdp','tp'}, use_global_device_ids=true, to_apply=%region_15.16 | all-reduce | flops 1792 | bytes 14336 | tf_op jit(solution)/shard_map/psum | solution.py:317
  671.1 2.2 fusion.27
  675.1 593.4 %all-reduce.7.cloned.1.call-done = f32[896,7296]{1,0:T(8,128)} async-done(((f32[896,7296]{1,0:T(8,128)}), f32[896,7296]{1,0:T(8,128)}) %all-reduce.7.cloned.1.call-update) | async-done | bytes 26148880
  1268.5 2.9 dynamic-slice_bitcast_fusion
  (215 shorter events, 30.9 us)
Async XLA Ops:
  8.0 138.9 %copy-start.36 = (bf16[448,56]{0,1:T(8,128)(2,1)S(1)}, bf16[448,56]{0,1:T(8,128)(2,1)}, u32[]{:S(2)}) copy-start(bf16[448,56]{0,1:T(8,128)(2,1)} %param.24) | copy-start | bytes 150532
  8.0 251.5 %reduce-scatter.5.cloned.1.call-start = ((), (), s32[]{:S(2)}) async-start(), calls=%async_computation.5 | async-start | bytes 688128 | tf_op jit(solution)/shard_map/reduce_scatter | solution.py:195
  8.1 180.8 %collective-permute-start.1 = (bf16[56,448]{1,0:T(8,128)(2,1)}, bf16[56,448]{1,0:T(8,128)(2,1)S(1)}, u32[]{:S(2)}, u32[]{:S(2)}) collective-permute-start(bf16[56,448]{1,0:T(8,128)(2,1)} %param.21), channel_id=1, source_target_pairs={{0,30},{2,0},{4,2},{6,4},{8,6},{10,8},{12,10},{14,12},{16,14},{18,... | collective-permute-start | bytes 150536 | tf_op jit(solution)/shard_map/ppermute | solution.py:26
  15.0 176.6 %collective-permute-start = (bf16[56,448]{1,0:T(8,128)(2,1)}, bf16[56,448]{1,0:T(8,128)(2,1)S(1)}, u32[]{:S(2)}, u32[]{:S(2)}) collective-permute-start(bf16[56,448]{1,0:T(8,128)(2,1)} %param.21), channel_id=1, source_target_pairs={{0,2},{2,4},{4,6},{6,8},{8,10},{10,12},{12,14},{14,16},{16,18},{18... | collective-permute-start | bytes 150536 | tf_op jit(solution)/shard_map/ppermute | solution.py:21
  15.1 172.7 %copy-start.44 = (f32[32]{0:T(128)}, f32[32]{0:T(128)S(1)}, u32[]{:S(2)}) copy-start(f32[32]{0:T(128)S(1)} %multiply_power_fusion) | copy-start | bytes 388
  15.1 172.7 %copy-start.40 = (f32[256]{0:T(256)}, f32[256]{0:T(256)S(1)}, u32[]{:S(2)}) copy-start(f32[256]{0:T(256)S(1)} %fusion.65) | copy-start | bytes 3076
  18.2 169.6 %copy-start.46 = (f32[128]{0:T(128)}, f32[128]{0:T(128)S(1)}, u32[]{:S(2)}) copy-start(f32[128]{0:T(128)S(1)} %add_rsqrt_fusion.1) | copy-start | bytes 1540
  64.9 75.9 %copy-start.28 = (f32[896]{0:T(1024)}, f32[896]{0:T(1024)S(1)}, u32[]{:S(2)}) copy-start(f32[896]{0:T(1024)S(1)} %convert_element_type.200) | copy-start | bytes 10756
  101.8 44.2 %copy-start.10 = (bf16[896,64]{1,0:T(8,128)(2,1)}, bf16[896,64]{1,0:T(8,128)(2,1)S(1)}, u32[]{:S(2)}) copy-start(bf16[896,64]{1,0:T(8,128)(2,1)S(1)} %all_gather.47) | copy-start | bytes 344068
  140.8 6.1 copy-start.12
  144.1 43.8 %copy-start.35 = (bf16[56,448]{1,0:T(8,128)(2,1)S(1)}, bf16[56,448]{1,0:T(8,128)(2,1)}, u32[]{:S(2)}) copy-start(bf16[56,448]{1,0:T(8,128)(2,1)} %param.21) | copy-start | bytes 150532
  146.1 101.3 %copy-start.21 = (f32[256,32]{0,1:T(8,128)}, f32[256,32]{0,1:T(8,128)S(1)}, u32[]{:S(2)}) copy-start(f32[256,32]{0,1:T(8,128)S(1)} %get-tuple-element.65) | copy-start | bytes 98308
  146.9 101.0 %copy-start.30 = (bf16[256,32]{0,1:T(8,128)(2,1)}, bf16[256,32]{0,1:T(8,128)(2,1)S(1)}, u32[]{:S(2)}) copy-start(bf16[256,32]{0,1:T(8,128)(2,1)S(1)} %get-tuple-element.61) | copy-start | bytes 49156
  188.8 4.9 collective-permute-start.3
  191.7 7.8 collective-permute-start.2
  193.7 7.6 collective-permute-start.5
  199.5 7.9 collective-permute-start.4
  201.3 7.8 collective-permute-start.7
  207.4 7.9 collective-permute-start.6
  207.4 40.5 %copy-start.32 = (bf16[256,32]{0,1:T(8,128)(2,1)S(1)}, bf16[256,32]{0,1:T(8,128)(2,1)}, u32[]{:S(2)}) copy-start(bf16[256,32]{0,1:T(8,128)(2,1)} %get-tuple-element.62) | copy-start | bytes 49156
  207.4 40.4 %copy-start.34 = (pred[256,256]{0,1:T(8,128)(4,1)S(1)}, pred[256,256]{0,1:T(8,128)(4,1)}, u32[]{:S(2)}) copy-start(pred[256,256]{0,1:T(8,128)(4,1)} %fusion.36) | copy-start | bytes 196612
  209.1 7.8 collective-permute-start.9
  215.2 7.8 collective-permute-start.8
  216.9 7.8 collective-permute-start.11
  223.0 8.3 collective-permute-start.10
  224.6 14.5 %collective-permute-start.13 = (bf16[56,448]{1,0:T(8,128)(2,1)S(1)}, bf16[56,448]{1,0:T(8,128)(2,1)S(1)}, u32[]{:S(2)}, u32[]{:S(2)}) collective-permute-start(bf16[56,448]{1,0:T(8,128)(2,1)S(1)} %collective-permute-done.11), channel_id=1, source_target_pairs={{0,30},{2,0},{4,2},{6,4},{8,6},{10,8},{12,10},{14,12},{16,14},{18,... | collective-permute-start | bytes 150536 | tf_op jit(solution)/shard_map/ppermute | solution.py:26
  231.3 7.8 collective-permute-start.12
  239.1 7.8 collective-permute-start.14
  249.9 9.6 copy-start
  251.2 76.5 %all-gather.6.cloned.1.call-start = ((), (), s32[]{:S(2)}) async-start(), calls=%async_computation.7 | async-start | bytes 4630528 | tf_op jit(solution)/shard_map/all_gather | solution.py:95
  251.8 154.6 %all-gather.4.cloned.1.call-start = ((), (), s32[]{:S(2)}) async-start(), calls=%async_computation.6 | async-start | bytes 4630528 | tf_op jit(solution)/shard_map/all_gather | solution.py:94
  252.4 232.7 %all-gather.8.cloned.1.call-start = ((), (), s32[]{:S(2)}) async-start(), calls=%async_computation.8 | async-start | bytes 4630528 | tf_op jit(solution)/shard_map/all_gather | solution.py:96
  253.0 256.3 %reduce-scatter.9.cloned.1.call-start = ((), (), s32[]{:S(2)}) async-start(), calls=%async_computation.10 | async-start | bytes 688128 | tf_op jit(solution)/shard_map/reduce_scatter | solution.py:229
  485.1 6.9 copy-start.50
  498.1 63.5 %reduce-scatter.11.cloned.1.call-start = ((), (), s32[]{:S(2)}) async-start(), calls=%async_computation.11 | async-start | bytes 688128 | tf_op jit(solution)/shard_map/reduce_scatter | solution.py:292
  498.2 6.3 copy-start.3
  498.2 6.3 copy-start.15
  520.8 150.3 %reduce-scatter.7.cloned.1.call-start = ((), (), s32[]{:S(2)}) async-start(), calls=%async_computation.9 | async-start | bytes 688128 | tf_op jit(solution)/shard_map/reduce_scatter | solution.py:212
  532.0 736.5 %all-reduce.7.cloned.1.call-start = ((), (), s32[]{:S(2)}) async-start(), calls=%async_computation.12 | async-start | bytes 52297728
  556.4 5.2 copy-start.47
  556.4 6.4 copy-start.39
  556.4 114.6 %copy-start.4 = (bf16[128,896]{1,0:T(8,128)(2,1)S(1)}, bf16[128,896]{1,0:T(8,128)(2,1)}, u32[]{:S(2)}) copy-start(bf16[128,896]{1,0:T(8,128)(2,1)} %reduce-scatter.5.cloned.1.call-done) | copy-start | bytes 688132
  556.4 114.6 %copy-start.8 = (bf16[128,896]{1,0:T(8,128)(2,1)S(1)}, bf16[128,896]{1,0:T(8,128)(2,1)}, u32[]{:S(2)}) copy-start(bf16[128,896]{1,0:T(8,128)(2,1)} %param.18) | copy-start | bytes 688132
  556.4 114.6 %copy-start.9 = (bf16[128,896]{1,0:T(8,128)(2,1)S(1)}, bf16[128,896]{1,0:T(8,128)(2,1)}, u32[]{:S(2)}) copy-start(bf16[128,896]{1,0:T(8,128)(2,1)} %reduce-scatter.9.cloned.1.call-done) | copy-start | bytes 688132
  556.5 114.6 %copy-start.27 = (f32[896]{0:T(1024)S(1)}, f32[896]{0:T(1024)}, u32[]{:S(2)}) copy-start(f32[896]{0:T(1024)} %convert_element_type.213) | copy-start | bytes 10756
  556.5 114.6 %copy-start.43 = (f32[128]{0:T(128)S(1)}, f32[128]{0:T(128)}, u32[]{:S(2)}) copy-start(f32[128]{0:T(128)} %copy-done.42) | copy-start | bytes 1540
  556.5 114.6 %copy-start.49 = (f32[128]{0:T(128)S(1)}, f32[128]{0:T(128)}, u32[]{:S(2)}) copy-start(f32[128]{0:T(128)} %copy-done.48) | copy-start | bytes 1540
  556.5 116.8 %all-to-all-start = ((bf16[16,56,1024]{2,1,0:T(8,128)(2,1)}), bf16[16,56,1024]{2,1,0:T(8,128)(2,1)S(1)}, u32[]{:S(2)}, u32[]{:S(2)}) async-start(bf16[16,56,1024]{2,1,0:T(8,128)(2,1)} %pad_maximum_fusion.1), calls=%async_computation.4 | async-start | bytes 3670016 | tf_op jit(solution)/shard_map/all_to_all | solution.py:41
  (27 other events, 40.9 us)
Sparse Core Ops, SparseCore 0:
  251.3 3.7 reduce-scatter.4
  498.2 6.4 reduce-scatter.8
  520.9 6.4 reduce-scatter.10
  532.1 7.1 reduce-scatter.6
Sparse Core Ops, SparseCore 1:
  254.7 72.9 all-gather.5
  330.6 75.7 all-gather.3
  409.3 75.7 all-gather.7
  551.8 716.6 all-reduce.6
